TPU v7x, 32 devices: a whole 2x2x4 slice. The times are simulated.
32 devices in a mesh: gx: 8 (over z, y), ha: 4 (over x, core).
Axes of the slice: x: 2, y: 2, z: 4, core: 2. Of those that a mesh axis runs over, the one named last changes fastest.
Arguments:
- value_field: float32 [8, 32, 16, 16], P('ha', None, 'gx'), may hold values from -6 to 6
- avoid_field: float32 [8, 32, 16, 16], P('ha', None, 'gx'), may hold values from -6 to 6
- sample_adjoint: float32 [8, 4, 8, 128], P('gx', 'ha'), may hold values from -6 to 6
- offset_y: float32 [8, 4, 8, 128], P('gx', 'ha'), may hold values from 0 to 1
- offset_s: float32 [8, 4, 8, 128], P('gx', 'ha'), may hold values from 0 to 1
- start_xy: int32 [8, 4, 8, 128], P('gx', 'ha'), may hold values from 0 to 30, as said below
- start_hs: int32 [8, 4, 8, 128], P('gx', 'ha'), may hold values from 0 to 62, as said below
- send_counts: int32 [8, 4, 8], P('gx', 'ha'), may hold values from 16 to 128, as said below
Outputs:
- next_value: float32 [8, 32, 16, 16], P('ha', None, 'gx')
- value_grad: float32 [8, 32, 16, 16], P('ha', None, 'gx')
- avoid_grad: float32 [8, 32, 16, 16], P('ha', None, 'gx')
Inputs may be any that keep to these rules, and one draw needn't show every extreme that they name: `start_xy`: the y cell of a start is at most 14. `start_hs`: the speed cell of a start is at most 30. `send_counts`: the live slots of a row are its first ones. For each index along ha, one owner drawn from the seed gets all 128 slots live from every sender.
All inputs are finite; a program needn't handle non-finite values.
Results may differ from a plain program's by a relative error of at most 0.00002.
Values sent between devices are 32-bit elements; how exact they have to be, the bound alone decides.
A program may use at most 64 MiB of HBM per device.

v0:
```python
import math

import jax
import jax.numpy as jnp
from jax import lax
from jax.sharding import PartitionSpec as P

TIME_STEP = 0.3
SHARPNESS = 2.0
SOFTENING = 0.1
TURN_RATE = 0.5
ACCELERATION = 0.3
SLOWEST = 0.2
SPEED_RANGE = 0.8
FASTEST = 1.0


def with_halo(block, sides, width):
    for axis, dim in sides:
        count = lax.axis_size(axis)
        forward = [(i, i + 1) for i in range(count - 1)]
        forward.append((count - 1, 0))
        backward = [(target, source) for source, target in forward]
        low = lax.ppermute(
            lax.slice_in_dim(block, block.shape[dim] - width, None, axis=dim), axis, forward
        )
        high = lax.ppermute(lax.slice_in_dim(block, 0, width, axis=dim), axis, backward)
        block = jnp.concatenate([low, block, high], axis=dim)
    return block


def smooth_abs(slope_value):
    return jnp.sqrt(slope_value * slope_value + SOFTENING * SOFTENING)


def edge_neighbours(grid_field, along_dim):
    length = grid_field.shape[along_dim]
    first_plane = lax.slice_in_dim(grid_field, 0, 1, axis=along_dim)
    last_plane = lax.slice_in_dim(grid_field, length - 1, length, axis=along_dim)
    upper_cells = jnp.concatenate(
        [lax.slice_in_dim(grid_field, 1, length, axis=along_dim), last_plane], along_dim
    )
    lower_cells = jnp.concatenate(
        [first_plane, lax.slice_in_dim(grid_field, 0, length - 1, axis=along_dim)], along_dim
    )
    return (upper_cells, lower_cells)


def linear_term(grid_field, upper_cells, lower_cells, factor):
    return (
        factor * (upper_cells - lower_cells) * 0.5
        - FASTEST * (upper_cells - 2.0 * grid_field + lower_cells) * 0.5
    )


def turn_term(grid_field, upper_cells, lower_cells, turn_rate):
    return turn_rate * smooth_abs(0.5 * (upper_cells - lower_cells)) - turn_rate * 0.5 * (
        upper_cells - 2.0 * grid_field + lower_cells
    )


def coefficients(head_index, total_heads, speeds):
    heading_angle = 2.0 * math.pi / total_heads * head_index.astype(jnp.float32)
    speed_cell = SLOWEST + SPEED_RANGE * jnp.arange(speeds, dtype=jnp.int32).astype(jnp.float32) / (
        speeds - 1
    )
    along_x = jnp.cos(heading_angle)[:, None, None, None] * speed_cell[None, :, None, None]
    along_y = jnp.sin(heading_angle)[:, None, None, None] * speed_cell[None, :, None, None]
    return (along_x, along_y)


def to_columns(grid_field):
    return jnp.swapaxes(
        lax.all_to_all(grid_field, "gx", split_axis=3, concat_axis=2, tiled=True), 2, 3
    )


def from_columns(grid_field):
    return lax.all_to_all(
        jnp.swapaxes(grid_field, 2, 3), "gx", split_axis=2, concat_axis=3, tiled=True
    )


def corner_weights(weight, offset_rows, offset_speed):
    return [
        weight * (1.0 - offset_rows) * (1.0 - offset_speed),
        weight * offset_rows * (1.0 - offset_speed),
        weight * (1.0 - offset_rows) * offset_speed,
        weight * offset_rows * offset_speed,
    ]


def on_device(
    value_field, avoid_field, sample_adjoint, offset_y, offset_s, start_xy, start_hs, send_counts
):
    head_count, speeds, row_count, line_count = value_field.shape
    groups = lax.axis_size("gx")
    slot_count = sample_adjoint.shape[3]
    head_index = lax.axis_index("ha") * head_count + jnp.arange(head_count, dtype=jnp.int32)
    along_x, along_y = coefficients(head_index, head_count * lax.axis_size("ha"), speeds)
    padded = with_halo(value_field, (("ha", 0),), 1)
    ahead_plane = padded[2:]
    behind = padded[:-2]
    slope_turn = 0.5 * (ahead_plane - behind)
    turning = TURN_RATE * smooth_abs(slope_turn) - TURN_RATE * 0.5 * (
        ahead_plane - 2.0 * value_field + behind
    )

    def local_terms(grid_field):
        upper_cells, lower_cells = edge_neighbours(grid_field, 3)
        summed = linear_term(grid_field, upper_cells, lower_cells, along_y)
        upper_cells, lower_cells = edge_neighbours(grid_field, 1)
        return summed + turn_term(grid_field, upper_cells, lower_cells, ACCELERATION)

    local_part, local_back = jax.vjp(local_terms, value_field)

    def line_term(grid_field):
        upper_cells, lower_cells = edge_neighbours(grid_field, 3)
        return linear_term(grid_field, upper_cells, lower_cells, along_x)

    across, line_back = jax.vjp(line_term, to_columns(value_field))
    across = from_columns(across)
    hamilton = across + local_part + turning
    relaxed = value_field - TIME_STEP * hamilton
    excess = SHARPNESS * (relaxed - avoid_field)
    next_value = avoid_field + jax.nn.softplus(excess) / SHARPNESS
    blend_share = jax.nn.sigmoid(excess)
    counts = send_counts.reshape(groups)
    live_slot = jnp.arange(slot_count, dtype=jnp.int32)[None, :] < counts[:, None]
    weight = jnp.where(live_slot, sample_adjoint.reshape(groups, slot_count), 0.0)
    offset_rows = offset_y.reshape(groups, slot_count)
    offset_speed = offset_s.reshape(groups, slot_count)
    cell_rows = start_xy.reshape(groups, slot_count)
    states = start_hs.reshape(groups, slot_count)
    payload = jnp.concatenate(corner_weights(weight, offset_rows, offset_speed), axis=1)
    payload, cell_rows, states = (
        lax.all_to_all(payload, "gx", split_axis=0, concat_axis=0, tiled=True),
        lax.all_to_all(cell_rows, "gx", split_axis=0, concat_axis=0, tiled=True),
        lax.all_to_all(states, "gx", split_axis=0, concat_axis=0, tiled=True),
    )
    pieces = jnp.split(payload, 4, axis=1)
    plane = row_count * line_count
    flat_index = states * plane + cell_rows
    cell_index = jnp.concatenate(
        [flat_index, flat_index + 1, flat_index + plane, flat_index + plane + 1], axis=0
    )
    deposit_sum = jnp.zeros((head_count * speeds * plane,), jnp.float32)
    deposit_sum = deposit_sum.at[cell_index.reshape(-1)].add(
        jnp.concatenate(pieces, axis=0).reshape(-1)
    )
    adjoint = deposit_sum.reshape(value_field.shape)
    avoid_grad = adjoint * (1.0 - blend_share)
    carried = adjoint * blend_share
    pull_turn = carried * TURN_RATE * slope_turn / smooth_abs(slope_turn)
    stacked = with_halo(jnp.stack([carried, pull_turn]), (("ha", 1),), 1)
    back_turn = 0.5 * (stacked[1, :-2] - stacked[1, 2:]) - TURN_RATE * 0.5 * (
        stacked[0, 2:] - 2.0 * carried + stacked[0, :-2]
    )
    back_local = local_back(carried)[0]
    back_across = from_columns(line_back(to_columns(carried))[0])
    value_grad = carried - TIME_STEP * (back_across + back_local + back_turn)
    return (next_value, value_grad, avoid_grad)


def solution(mesh):
    in_specs = (
        P("ha", None, "gx", None),
        P("ha", None, "gx", None),
        P("gx", "ha", None, None),
        P("gx", "ha", None, None),
        P("gx", "ha", None, None),
        P("gx", "ha", None, None),
        P("gx", "ha", None, None),
        P("gx", "ha", None),
    )
    out_specs = (P("ha", None, "gx", None), P("ha", None, "gx", None), P("ha", None, "gx", None))
    return jax.shard_map(
        on_device, mesh=mesh, in_specs=in_specs, out_specs=out_specs, check_vma=False
    )
```

profile of v0, /device:TPU:0, one launch (start us, length us, event | category | flops | bytes accessed | tf_op | source)
XLA Modules:
  0.0 99.7 jit_solution(10327407511817762513)
XLA Ops:
  0.6 7.3 %all-to-all-start.2 = ((s32[8,1,128]{2,1,0:T(1,128)}), s32[8,1,128]{2,1,0:T(1,128)S(1)}, u32[]{:S(2)}, u32[]{:S(2)}) async-start(s32[8,1,128]{2,1,0:T(1,128)} %bitcast.167), calls=%async_computation.2 | async-start | bytes 8192 | tf_op jit(solution)/shard_map/all_to_all | solution.py:139
  7.9 0.8 fusion.40
  8.7 0.7 collective-permute-start
  10.5 3.9 %all-to-all-done.2 = s32[8,1,128]{2,1,0:T(1,128)S(1)} async-done(((s32[8,1,128]{2,1,0:T(1,128)}), s32[8,1,128]{2,1,0:T(1,128)S(1)}, u32[]{:S(2)}, u32[]{:S(2)}) %all-to-all-start.2) | async-done | bytes 4128 | tf_op jit(solution)/shard_map/all_to_all | solution.py:139
  14.3 3.3 %all-to-all-start.3 = ((s32[8,1,128]{2,1,0:T(1,128)}), s32[8,1,128]{2,1,0:T(1,128)S(1)}, u32[]{:S(2)}, u32[]{:S(2)}) async-start(s32[8,1,128]{2,1,0:T(1,128)} %bitcast.11), calls=%async_computation.3 | async-start | bytes 8192 | tf_op jit(solution)/shard_map/all_to_all | solution.py:138
  17.7 0.6 all_to_all.84
  18.3 0.7 reshape.163
  19.0 5.0 %all-to-all-done.3 = s32[8,1,128]{2,1,0:T(1,128)S(1)} async-done(((s32[8,1,128]{2,1,0:T(1,128)}), s32[8,1,128]{2,1,0:T(1,128)S(1)}, u32[]{:S(2)}, u32[]{:S(2)}) %all-to-all-start.3) | async-done | bytes 4128 | tf_op jit(solution)/shard_map/all_to_all | solution.py:138
  24.0 3.3 %all-to-all-start = ((f32[8,1,256]{2,1,0:T(1,128)}), f32[8,1,256]{2,1,0:T(1,128)S(1)}, u32[]{:S(2)}, u32[]{:S(2)}) async-start(f32[8,1,256]{2,1,0:T(1,128)} %reshape.163), calls=%async_computation | async-start | bytes 16384 | tf_op jit(solution)/shard_map/all_to_all | solution.py:74
  27.4 6.4 %all-to-all-done = f32[8,1,256]{2,1,0:T(1,128)S(1)} async-done(((f32[8,1,256]{2,1,0:T(1,128)}), f32[8,1,256]{2,1,0:T(1,128)S(1)}, u32[]{:S(2)}, u32[]{:S(2)}) %all-to-all-start) | async-done | bytes 8224 | tf_op jit(solution)/shard_map/all_to_all | solution.py:74
  33.8 3.3 %all-to-all-start.4 = ((f32[8,1,512]{2,1,0:T(1,128)}), f32[8,1,512]{2,1,0:T(1,128)S(1)}, u32[]{:S(2)}, u32[]{:S(2)}) async-start(f32[8,1,512]{2,1,0:T(1,128)} %all_to_all.84), calls=%async_computation.4 | async-start | bytes 32768 | tf_op jit(solution)/shard_map/all_to_all | solution.py:137
  37.7 0.7 reduce
  38.6 0.7 reshape.165
  39.3 4.3 %all-to-all-done.4 = f32[8,1,512]{2,1,0:T(1,128)S(1)} async-done(((f32[8,1,512]{2,1,0:T(1,128)}), f32[8,1,512]{2,1,0:T(1,128)S(1)}, u32[]{:S(2)}, u32[]{:S(2)}) %all-to-all-start.4) | async-done | bytes 16416 | tf_op jit(solution)/shard_map/all_to_all | solution.py:137
  43.6 3.3 %all-to-all-start.1 = ((f32[8,1,256]{2,1,0:T(1,128)}), f32[8,1,256]{2,1,0:T(1,128)S(1)}, u32[]{:S(2)}, u32[]{:S(2)}) async-start(f32[8,1,256]{2,1,0:T(1,128)} %reshape.165), calls=%async_computation.1 | async-start | bytes 16384 | tf_op jit(solution)/shard_map/all_to_all | solution.py:79
  47.0 22.1 %scatter_custom_fusion = f32[2048]{0:T(1024)S(1)} fusion(s32[4096]{0:T(1024)S(1)} %bitcast.166, f32[4096]{0:T(1024)S(1)} %maximum_bitcast_fusion, f32[]{:T(128)} %constant.18.clone.1), kind=kCustom, calls=%fused_computation.78 | custom fusion | flops 4096 | bytes 8196 | tf_op jit(solution)/shard_map/scatter-add | solution.py:148
  69.3 0.7 reduce.1
  70.2 0.7 copy-done.1
  70.9 0.8 subtract_multiply_fusion
  71.7 0.7 negate_add_fusion.1
  72.3 0.7 reshape.167
  73.0 5.8 %all-to-all-start.5 = ((f32[8,1,256]{2,1,0:T(1,128)}), f32[8,1,256]{2,1,0:T(1,128)S(1)}, u32[]{:S(2)}, u32[]{:S(2)}) async-start(f32[8,1,256]{2,1,0:T(1,128)} %reshape.167), calls=%async_computation.5 | async-start | bytes 16384 | tf_op jit(solution)/shard_map/all_to_all | solution.py:74
  78.9 6.5 %all-to-all-done.5 = f32[8,1,256]{2,1,0:T(1,128)S(1)} async-done(((f32[8,1,256]{2,1,0:T(1,128)}), f32[8,1,256]{2,1,0:T(1,128)S(1)}, u32[]{:S(2)}, u32[]{:S(2)}) %all-to-all-start.5) | async-done | bytes 8224 | tf_op jit(solution)/shard_map/all_to_all | solution.py:74
  85.3 0.7 reduce.2
  86.2 0.6 copy-done.5
  87.0 0.7 reshape.169
  87.7 3.3 %all-to-all-start.6 = ((f32[8,1,256]{2,1,0:T(1,128)}), f32[8,1,256]{2,1,0:T(1,128)S(1)}, u32[]{:S(2)}, u32[]{:S(2)}) async-start(f32[8,1,256]{2,1,0:T(1,128)} %reshape.169), calls=%async_computation.6 | async-start | bytes 16384 | tf_op jit(solution)/shard_map/all_to_all | solution.py:79
  91.1 1.7 %collective-permute-start.3 = (f32[2,1,32,2,16]{2,4,3,1,0:T(8,128)S(1)}, f32[2,1,32,2,16]{2,4,3,1,0:T(8,128)S(1)}, u32[]{:S(2)}, u32[]{:S(2)}) collective-permute-start(f32[2,1,32,2,16]{2,4,3,1,0:T(8,128)S(1)} %get-tuple-element.11), channel_id=1, source_target_pairs={{1,0},{2,1},{3,2},{0,3},{5,4},{6,5},{7,6},{4,7},{9,8},{10,9},{11,1... | collective-permute-start | bytes 24584 | tf_op jit(solution)/shard_map/ppermute | solution.py:27
  93.0 4.5 %all-to-all-done.6 = f32[8,1,256]{2,1,0:T(1,128)S(1)} async-done(((f32[8,1,256]{2,1,0:T(1,128)}), f32[8,1,256]{2,1,0:T(1,128)S(1)}, u32[]{:S(2)}, u32[]{:S(2)}) %all-to-all-start.6) | async-done | bytes 8224 | tf_op jit(solution)/shard_map/all_to_all | solution.py:79
  97.5 0.7 reduce.3
  98.4 0.6 copy-done.7
  99.0 0.7 fusion.9
  (67 shorter events, 2.8 us)
Async XLA Ops:
  0.6 13.7 %all-to-all-start.2 = ((s32[8,1,128]{2,1,0:T(1,128)}), s32[8,1,128]{2,1,0:T(1,128)S(1)}, u32[]{:S(2)}, u32[]{:S(2)}) async-start(s32[8,1,128]{2,1,0:T(1,128)} %bitcast.167), calls=%async_computation.2 | async-start | bytes 8192 | tf_op jit(solution)/shard_map/all_to_all | solution.py:139
  7.9 1.5 %copy-start = (f32[2,32,2,16]{1,3,2,0:T(8,128)S(1)}, f32[2,32,2,16]{1,3,2,0:T(8,128)}, u32[]{:S(2)}) copy-start(f32[2,32,2,16]{1,3,2,0:T(8,128)} %param.8) | copy-start | bytes 24580
  8.7 61.5 %collective-permute-start = (f32[1,32,2,16]{1,3,2,0:T(8,128)S(1)}, f32[1,32,2,16]{1,3,2,0:T(8,128)S(1)}, u32[]{:S(2)}, u32[]{:S(2)}) collective-permute-start(f32[1,32,2,16]{1,3,2,0:T(8,128)S(1)} %get-tuple-element.34), channel_id=1, source_target_pairs={{1,0},{2,1},{3,2},{0,3},{5,4},{6,5},{7,6},{4,7},{9,8},{10,9},{11,1... | collective-permute-start | bytes 12296 | tf_op jit(solution)/shard_map/ppermute | solution.py:27
  9.4 60.8 %collective-permute-start.1 = (f32[1,32,2,16]{1,3,2,0:T(8,128)S(1)}, f32[1,32,2,16]{1,3,2,0:T(8,128)S(1)}, u32[]{:S(2)}, u32[]{:S(2)}) collective-permute-start(f32[1,32,2,16]{1,3,2,0:T(8,128)S(1)} %get-tuple-element.35), channel_id=1, source_target_pairs={{0,1},{1,2},{2,3},{3,0},{4,5},{5,6},{6,7},{7,4},{8,9},{9,10},{10,1... | collective-permute-start | bytes 12296 | tf_op jit(solution)/shard_map/ppermute | solution.py:24
  9.5 0.7 copy-start.4
  9.6 0.7 copy-start.3
  9.6 0.7 copy-start.2
  9.6 0.7 copy-start.6
  14.3 9.6 %all-to-all-start.3 = ((s32[8,1,128]{2,1,0:T(1,128)}), s32[8,1,128]{2,1,0:T(1,128)S(1)}, u32[]{:S(2)}, u32[]{:S(2)}) async-start(s32[8,1,128]{2,1,0:T(1,128)} %bitcast.11), calls=%async_computation.3 | async-start | bytes 8192 | tf_op jit(solution)/shard_map/all_to_all | solution.py:138
  24.0 9.8 %all-to-all-start = ((f32[8,1,256]{2,1,0:T(1,128)}), f32[8,1,256]{2,1,0:T(1,128)S(1)}, u32[]{:S(2)}, u32[]{:S(2)}) async-start(f32[8,1,256]{2,1,0:T(1,128)} %reshape.163), calls=%async_computation | async-start | bytes 16384 | tf_op jit(solution)/shard_map/all_to_all | solution.py:74
  33.8 9.9 %all-to-all-start.4 = ((f32[8,1,512]{2,1,0:T(1,128)}), f32[8,1,512]{2,1,0:T(1,128)S(1)}, u32[]{:S(2)}, u32[]{:S(2)}) async-start(f32[8,1,512]{2,1,0:T(1,128)} %all_to_all.84), calls=%async_computation.4 | async-start | bytes 32768 | tf_op jit(solution)/shard_map/all_to_all | solution.py:137
  43.6 25.7 %all-to-all-start.1 = ((f32[8,1,256]{2,1,0:T(1,128)}), f32[8,1,256]{2,1,0:T(1,128)S(1)}, u32[]{:S(2)}, u32[]{:S(2)}) async-start(f32[8,1,256]{2,1,0:T(1,128)} %reshape.165), calls=%async_computation.1 | async-start | bytes 16384 | tf_op jit(solution)/shard_map/all_to_all | solution.py:79
  70.1 0.8 copy-start.1
  73.0 12.3 %all-to-all-start.5 = ((f32[8,1,256]{2,1,0:T(1,128)}), f32[8,1,256]{2,1,0:T(1,128)S(1)}, u32[]{:S(2)}, u32[]{:S(2)}) async-start(f32[8,1,256]{2,1,0:T(1,128)} %reshape.167), calls=%async_computation.5 | async-start | bytes 16384 | tf_op jit(solution)/shard_map/all_to_all | solution.py:74
  86.2 0.7 copy-start.5
  87.7 9.8 %all-to-all-start.6 = ((f32[8,1,256]{2,1,0:T(1,128)}), f32[8,1,256]{2,1,0:T(1,128)S(1)}, u32[]{:S(2)}, u32[]{:S(2)}) async-start(f32[8,1,256]{2,1,0:T(1,128)} %reshape.169), calls=%async_computation.6 | async-start | bytes 16384 | tf_op jit(solution)/shard_map/all_to_all | solution.py:79
  91.0 7.3 %collective-permute-start.2 = (f32[2,1,32,2,16]{2,4,3,1,0:T(8,128)S(1)}, f32[2,1,32,2,16]{2,4,3,1,0:T(8,128)S(1)}, u32[]{:S(2)}, u32[]{:S(2)}) collective-permute-start(f32[2,1,32,2,16]{2,4,3,1,0:T(8,128)S(1)} %get-tuple-element.12), channel_id=1, source_target_pairs={{0,1},{1,2},{2,3},{3,0},{4,5},{5,6},{6,7},{7,4},{8,9},{9,10},{10,1... | collective-permute-start | bytes 24584 | tf_op jit(solution)/shard_map/ppermute | solution.py:24
  91.1 7.2 %collective-permute-start.3 = (f32[2,1,32,2,16]{2,4,3,1,0:T(8,128)S(1)}, f32[2,1,32,2,16]{2,4,3,1,0:T(8,128)S(1)}, u32[]{:S(2)}, u32[]{:S(2)}) collective-permute-start(f32[2,1,32,2,16]{2,4,3,1,0:T(8,128)S(1)} %get-tuple-element.11), channel_id=1, source_target_pairs={{1,0},{2,1},{3,2},{0,3},{5,4},{6,5},{7,6},{4,7},{9,8},{10,9},{11,1... | collective-permute-start | bytes 24584 | tf_op jit(solution)/shard_map/ppermute | solution.py:27
  98.3 0.7 copy-start.7
where the time goes:
time: 101 us; the launch traced here: 99.7 us
  starting transfers between devices  32.2 us (32%)
  waiting for transfers between devices  30.5 us (30%)
  other arithmetic  27.5 us (27%)
  local copies, waits for them, and re-layouts  8.55 us (8%)
  between operations  1.07 us (1%)
    scatter-add x1, other arithmetic, on_device(): deposit_sum.at[cell_index.reshape(-1)]  22.1 us
    all_to_all x2, waiting for transfers between devices, to_columns(): lax.all_to_all(grid_field, 'gx', split_axis=3, concat_axis=2, tiled=True)  12.9 us
    all_to_all x2, starting transfers between devices, to_columns(): lax.all_to_all(grid_field, 'gx', split_axis=3, concat_axis=2, tiled=True)  9.11 us
    all_to_all x1, starting transfers between devices, on_device(): lax.all_to_all(states, 'gx', split_axis=0, concat_axis=0, tiled=True)  7.29 us
    all_to_all x2, starting transfers between devices, from_columns(): lax.all_to_all(jnp.swapaxes(grid_field, 2, 3), 'gx', split_axis=2, concat...  6.67 us
    unnamed x26, local copies, waits for them, and re-layouts  5.85 us
    all_to_all x1, waiting for transfers between devices, on_device(): lax.all_to_all(cell_rows, 'gx', split_axis=0, concat_axis=0, tiled=True)  4.97 us
    all_to_all x2, waiting for transfers between devices, from_columns(): lax.all_to_all(jnp.swapaxes(grid_field, 2, 3), 'gx', split_axis=2, concat...  4.47 us
  transfers between devices with their start and end apart: 11, of which 6 were waited for; matrix products, arithmetic and copies ran while one was open for 28% of the time, Pallas kernels for 0%

commit v1 on v0

v1 whole, which is shorter than its diff:
```python
import functools
import math

import jax
import jax.numpy as jnp
import numpy as np
from jax import lax
from jax.experimental import pallas as pl
from jax.experimental.pallas import tpu as pltpu
from jax.sharding import PartitionSpec as P

TIME_STEP = 0.3
SHARPNESS = 2.0
SOFTENING = 0.1
TURN_RATE = 0.5
ACCELERATION = 0.3
SLOWEST = 0.2
SPEED_RANGE = 0.8
ROWS = 8
MESH = pl.DeviceIdType.MESH


def smooth_abs(slope):
    return jnp.sqrt(slope * slope + SOFTENING * SOFTENING)


def upper(plane, axis):
    n = plane.shape[axis]
    return jnp.concatenate(
        [lax.slice_in_dim(plane, 1, n, axis=axis), lax.slice_in_dim(plane, n - 1, n, axis=axis)], axis
    )


def lower(plane, axis):
    n = plane.shape[axis]
    return jnp.concatenate(
        [lax.slice_in_dim(plane, 0, 1, axis=axis), lax.slice_in_dim(plane, 0, n - 1, axis=axis)], axis
    )


def spread(up, down, axis):
    n = up.shape[axis]
    from_lower = jnp.concatenate(
        [lax.slice_in_dim(down, 0, 1, axis=axis), lax.slice_in_dim(up, 0, n - 1, axis=axis)], axis
    )
    from_upper = jnp.concatenate(
        [lax.slice_in_dim(down, 1, n, axis=axis), lax.slice_in_dim(up, n - 1, n, axis=axis)], axis
    )
    return from_lower + from_upper


def pick(table, index):
    chosen = jnp.float32(table[0])
    for i in range(1, len(table)):
        chosen = jnp.where(index == i, jnp.float32(table[i]), chosen)
    return chosen


def kernel(
    groups, blocks,
    value_h, avoid_h, weight_h, offy_h, offs_h, xy_h, hs_h, count_h,
    next_o, vgrad_o, agrad_o,
    value, avoid, weight, offy, offs, xy, hs, count,
    pay, got, xhalo, hhalo, carried, turned, cxhalo, chhalo,
    in_sem, pay_send, pay_recv, x_send, x_recv, h_send, h_recv,
    cx_send, cx_recv, ch_send, ch_recv, self_sem,
):
    heads, cells, lines, speeds = value.shape
    slots = weight.shape[1]
    me = lax.axis_index("gx")
    hb = lax.axis_index("ha")
    h_next = lax.rem(hb + 1, blocks)
    h_prev = lax.rem(hb + blocks - 1, blocks)
    has_prev = me > 0
    has_next = me < groups - 1

    barrier = pltpu.get_barrier_semaphore()

    def greet(d):
        pl.semaphore_signal(
            barrier, inc=1, device_id=(lax.rem(me + d, groups), hb), device_id_type=MESH
        )

    if groups <= 8:
        for d in range(1, groups):
            greet(d)
    else:
        pl.loop(1, groups)(greet)
    for other in (h_prev, h_next):
        pl.semaphore_signal(barrier, inc=1, device_id=(me, other), device_id_type=MESH)

    pairs = (
        (weight_h, weight), (offy_h, offy), (offs_h, offs), (xy_h, xy), (hs_h, hs), (count_h, count),
        (value_h, value), (avoid_h, avoid),
    )
    loads = [pltpu.make_async_copy(a, b, in_sem.at[i]) for i, (a, b) in enumerate(pairs)]
    for load in loads:
        load.start()
    for load in loads[:6]:
        load.wait()

    owners = lax.broadcasted_iota(jnp.int32, (groups, groups), 0)
    lanes = lax.broadcasted_iota(jnp.int32, (groups, groups), 1)
    live = jnp.sum(
        jnp.where(owners == lanes, jnp.broadcast_to(count[...], (groups, groups)), 0).astype(jnp.float32),
        axis=1, keepdims=True,
    )
    slot = lax.broadcasted_iota(jnp.int32, (groups, slots), 1).astype(jnp.float32)
    w = jnp.where(slot < live, weight[...], 0.0)
    oy = offy[...]
    os = offs[...]
    state = hs[...]
    head = lax.div(state, speeds)
    pay[:, 0, :] = w * (1.0 - oy)
    pay[:, 1, :] = w * oy
    pay[:, 2, :] = 1.0 - os
    pay[:, 3, :] = os
    pay[:, 4, :] = (head * (cells * lines) + xy[...]).astype(jnp.float32)
    pay[:, 5, :] = (state - head * speeds).astype(jnp.float32)
    pay[:, 6, :] = jnp.zeros((groups, slots), jnp.float32)
    pay[:, 7, :] = jnp.zeros((groups, slots), jnp.float32)

    pl.semaphore_wait(barrier, groups - 1 + 2)

    def h_copy(side):
        return pltpu.make_async_remote_copy(
            value_h.at[0 if side == 0 else heads - 1], hhalo.at[1 - side],
            h_send.at[side], h_recv.at[1 - side],
            device_id=(me, h_prev if side == 0 else h_next), device_id_type=MESH,
        )

    def x_copy(side):
        return pltpu.make_async_remote_copy(
            value_h.at[:, 0 if side == 0 else cells - 1], xhalo.at[1 - side],
            x_send.at[side], x_recv.at[1 - side],
            device_id=(me - 1 if side == 0 else me + 1, hb), device_id_type=MESH,
        )

    def pay_copy(d):
        peer = lax.rem(me + d, groups)
        return pltpu.make_async_remote_copy(
            pay.at[peer], got.at[d], pay_send.at[d], pay_recv.at[d],
            device_id=(peer, hb), device_id_type=MESH,
        )

    for side in range(2):
        h_copy(side).start()
    for side, has in ((0, has_prev), (1, has_next)):
        @pl.when(has)
        def _():
            x_copy(side).start()

    if groups <= 8:
        for d in range(groups - 1, 0, -1):
            pay_copy(d).start()
    else:
        pl.loop(1, groups)(lambda d: pay_copy(d).start())
    mine = pltpu.make_async_copy(pay.at[me], got.at[0], self_sem)
    mine.start()
    loads[6].wait()
    loads[7].wait()

    for side, has in ((0, has_prev), (1, has_next)):
        @pl.when(jnp.logical_not(has))
        def _():
            xhalo[side] = value[:, 0 if side == 0 else cells - 1]

    total = heads * blocks
    angles = [np.float32(2.0 * math.pi / total) * np.float32(k) for k in range(total)]
    cosines = [float(np.cos(a)) for a in angles]
    sines = [float(np.sin(a)) for a in angles]
    speed = SLOWEST + SPEED_RANGE * lax.broadcasted_iota(jnp.int32, (1, speeds), 1).astype(
        jnp.float32
    ) / (speeds - 1)
    cx = [pick(cosines, hb * heads + h) * speed for h in range(heads)]
    cy = [pick(sines, hb * heads + h) * speed for h in range(heads)]
    grid = [(h, x) for h in range(heads) for x in range(cells)]
    v = {(h, x): value[h, x] for h, x in grid}
    part, s_slope = {}, {}
    for h, x in grid:
        here = v[h, x]
        up, down = upper(here, 0), lower(here, 0)
        term = cy[h] * (up - down) * 0.5 - (up - 2.0 * here + down) * 0.5
        up, down = upper(here, 1), lower(here, 1)
        slope = 0.5 * (up - down)
        size = smooth_abs(slope)
        s_slope[h, x] = slope / size
        part[h, x] = term + ACCELERATION * size - ACCELERATION * 0.5 * (up - 2.0 * here + down)

    for side in range(2):
        h_copy(side).wait_recv()
    for side, has in ((0, has_prev), (1, has_next)):
        @pl.when(has)
        def _():
            x_copy(1 - side).wait_recv()
    for x in range(cells):
        v[-1, x] = hhalo[0, x]
        v[heads, x] = hhalo[1, x]
    for h in range(heads):
        v[h, -1] = xhalo[0, h]
        v[h, cells] = xhalo[1, h]

    share, h_slope = {}, {}
    for h, x in grid:
        here = v[h, x]
        up, down = v[h + 1, x], v[h - 1, x]
        slope = 0.5 * (up - down)
        size = smooth_abs(slope)
        h_slope[h, x] = slope / size
        turning = TURN_RATE * size - TURN_RATE * 0.5 * (up - 2.0 * here + down)
        up, down = v[h, x + 1], v[h, x - 1]
        across = cx[h] * (up - down) * 0.5 - (up - 2.0 * here + down) * 0.5
        relaxed = here - TIME_STEP * (across + part[h, x] + turning)
        floor = avoid[h, x]
        excess = SHARPNESS * (relaxed - floor)
        small = jnp.exp(-jnp.abs(excess))
        next_o[h, x] = floor + (jnp.maximum(excess, 0.0) + jnp.log1p(small)) / SHARPNESS
        inverse = 1.0 / (1.0 + small)
        positive = excess >= 0.0
        share[h, x] = (
            jnp.where(positive, 1.0, small) * inverse, jnp.where(positive, small, 1.0) * inverse
        )

    rows = heads * cells * lines
    row_id = lax.broadcasted_iota(jnp.int32, (rows, slots), 0).astype(jnp.float32)
    speed_id = lax.broadcasted_iota(jnp.int32, (speeds, slots), 0).astype(jnp.float32)

    def operands(d):
        one = got[d]
        cell = jnp.broadcast_to(one[4:5], (rows, slots))
        left = jnp.where(row_id == cell, one[0:1], jnp.where(row_id == cell + 1.0, one[1:2], 0.0))
        cell = jnp.broadcast_to(one[5:6], (speeds, slots))
        right = jnp.where(
            speed_id == cell, one[2:3], jnp.where(speed_id == cell + 1.0, one[3:4], 0.0)
        )
        return left, right

    def product(left, right):
        return lax.dot_general(
            left, right, (((1,), (1,)), ((), ())),
            precision=lax.Precision.HIGHEST, preferred_element_type=jnp.float32,
        )

    mine.wait()
    if groups <= 8:
        for d in range(1, groups):
            pay_copy(d).wait_recv()
        both = [operands(d) for d in range(groups)]
        deposit = product(
            jnp.concatenate([b[0] for b in both], 1), jnp.concatenate([b[1] for b in both], 1)
        )
    else:
        pl.loop(1, groups)(lambda d: pay_copy(d).wait_recv())
        deposit = lax.fori_loop(
            0, groups, lambda d, so_far: so_far + product(*operands(d)),
            jnp.zeros((rows, speeds), jnp.float32),
        )

    c = {}
    for n, (h, x) in enumerate(grid):
        adjoint = deposit[n * lines : (n + 1) * lines]
        c[h, x] = adjoint * share[h, x][0]
        carried[h, x] = c[h, x]
        agrad_o[h, x] = adjoint * share[h, x][1]
    ahead, back = {}, {}
    for h, x in grid:
        pull = (0.5 * TURN_RATE) * c[h, x] * h_slope[h, x]
        keep = (0.5 * TURN_RATE) * c[h, x]
        ahead[h, x] = pull - keep
        back[h, x] = -pull - keep
    for x in range(cells):
        turned[0, x] = back[0, x]
        turned[1, x] = ahead[heads - 1, x]

    def ch_copy(side):
        return pltpu.make_async_remote_copy(
            turned.at[side], chhalo.at[1 - side], ch_send.at[side], ch_recv.at[1 - side],
            device_id=(me, h_prev if side == 0 else h_next), device_id_type=MESH,
        )

    def cx_copy(side):
        return pltpu.make_async_remote_copy(
            carried.at[:, 0 if side == 0 else cells - 1], cxhalo.at[1 - side],
            cx_send.at[side], cx_recv.at[1 - side],
            device_id=(me - 1 if side == 0 else me + 1, hb), device_id_type=MESH,
        )

    for side, has in ((0, has_prev), (1, has_next)):
        @pl.when(has)
        def _():
            cx_copy(side).start()

        @pl.when(jnp.logical_not(has))
        def _():
            cxhalo[side] = jnp.zeros_like(cxhalo[side])
    for side in range(2):
        ch_copy(side).start()

    local = {}
    for h, x in grid:
        here = c[h, x]
        grad = spread((0.5 * cy[h] - 0.5) * here, (-0.5 * cy[h] - 0.5) * here, 0)
        pull = (0.5 * ACCELERATION) * here * s_slope[h, x]
        keep = (0.5 * ACCELERATION) * here
        grad = grad + spread(pull - keep, -pull - keep, 1)
        local[h, x] = grad + (2.0 + TURN_RATE + ACCELERATION) * here

    for side in range(2):
        ch_copy(side).wait_recv()
    for side, has in ((0, has_prev), (1, has_next)):
        @pl.when(has)
        def _():
            cx_copy(1 - side).wait_recv()
    for h, x in grid:
        grad = local[h, x]
        grad = grad + (ahead[h - 1, x] if h > 0 else chhalo[0, x])
        grad = grad + (back[h + 1, x] if h < heads - 1 else chhalo[1, x])
        low, high = 0.5 * cx[h] - 0.5, -0.5 * cx[h] - 0.5
        if x > 0:
            grad = grad + low * c[h, x - 1]
        else:
            grad = grad + jnp.where(has_prev, low * cxhalo[0, h], high * c[h, x])
        if x < cells - 1:
            grad = grad + high * c[h, x + 1]
        else:
            grad = grad + jnp.where(has_next, high * cxhalo[1, h], low * c[h, x])
        vgrad_o[h, x] = c[h, x] - TIME_STEP * grad

    for side in range(2):
        h_copy(side).wait_send()
        ch_copy(side).wait_send()
    for side, has in ((0, has_prev), (1, has_next)):
        @pl.when(has)
        def _():
            x_copy(side).wait_send()
            cx_copy(side).wait_send()
    if groups <= 8:
        for d in range(1, groups):
            pay_copy(d).wait_send()
    else:
        pl.loop(1, groups)(lambda d: pay_copy(d).wait_send())


def on_device(groups, blocks, value, avoid, weight, offy, offs, xy, hs, count):
    slots = weight.shape[3]
    value = jnp.transpose(value, (0, 2, 3, 1))
    avoid = jnp.transpose(avoid, (0, 2, 3, 1))
    weight, offy, offs, xy, hs = (a.reshape(groups, slots) for a in (weight, offy, offs, xy, hs))
    count = count.reshape(1, groups)
    heads, cells, lines, speeds = value.shape
    f32 = jnp.float32
    dma = pltpu.SemaphoreType.DMA
    field = pltpu.VMEM(value.shape, f32)
    x_pair = pltpu.VMEM((2, heads, lines, speeds), f32)
    h_pair = pltpu.VMEM((2, cells, lines, speeds), f32)
    outs = pl.pallas_call(
        functools.partial(kernel, groups, blocks),
        out_shape=[jax.ShapeDtypeStruct(value.shape, f32)] * 3,
        in_specs=[pl.BlockSpec(memory_space=pl.ANY)] * 8,
        out_specs=[pl.BlockSpec(memory_space=pltpu.VMEM)] * 3,
        scratch_shapes=[
            field, field,
            *[pltpu.VMEM((groups, slots), f32)] * 3,
            *[pltpu.VMEM((groups, slots), jnp.int32)] * 2,
            pltpu.VMEM((1, groups), jnp.int32),
            pltpu.VMEM((groups, ROWS, slots), f32), pltpu.VMEM((groups, ROWS, slots), f32),
            x_pair, h_pair, field, h_pair, x_pair, h_pair,
            dma((8,)), dma((groups,)), dma((groups,)),
            dma((2,)), dma((2,)), dma((2,)), dma((2,)),
            dma((2,)), dma((2,)), dma((2,)), dma((2,)), dma,
        ],
        compiler_params=pltpu.CompilerParams(collective_id=0, has_side_effects=True),
        name="step",
    )(value, avoid, weight, offy, offs, xy, hs, count)
    return tuple(jnp.transpose(o, (0, 3, 1, 2)) for o in outs)


def solution(mesh):
    field = P("ha", None, "gx", None)
    sample = P("gx", "ha", None, None)
    return jax.shard_map(
        functools.partial(on_device, mesh.shape["gx"], mesh.shape["ha"]),
        mesh=mesh,
        in_specs=(field, field, sample, sample, sample, sample, sample, P("gx", "ha", None)),
        out_specs=(field, field, field),
        check_vma=False,
    )
```

time: 101 us -> 17.2 us (0.17)
  starting transfers between devices: 32.2 us -> 0 us
  waiting for transfers between devices: 30.5 us -> 0 us
  other arithmetic: 27.5 us -> 0 us
  Pallas kernels: 0 us -> 13.5 us
  local copies, waits for them, and re-layouts: 8.55 us -> 2.77 us
    all_to_all x7 -> x0, waiting for transfers between devices: 30.5 us -> none  [the longest x2 12.9 us: to_columns(): lax.all_to_all(grid_field, 'gx', split_axis=3, concat_axis=2, tiled=True)]
    all_to_all x7 -> x0, starting transfers between devices: 29.7 us -> none  [the longest x2 9.11 us: to_columns(): lax.all_to_all(grid_field, 'gx', split_axis=3, concat_axis=2, tiled=True)]
    scatter-add x1 -> x0, other arithmetic: 22.1 us -> none  [on_device(): deposit_sum.at[cell_index.reshape(-1)]]
    pallas_call x0 -> x1, Pallas kernels: none -> 13.5 us  [on_device(): pl.pallas_call(functools.partial(kernel, groups, blocks), out_shape=[jax....]
    unnamed x26 -> x7, local copies, waits for them, and re-layouts: 5.85 us -> 2.77 us
    all_to_all x4 -> x0, other arithmetic: 2.84 us -> none  [the longest x2 1.43 us: from_columns(): lax.all_to_all(jnp.swapaxes(grid_field, 2, 3), 'gx', split_axis=2, concat...]
    ppermute x4 -> x0, starting transfers between devices: 2.44 us -> none  [the longest x2 2.38 us: with_halo(): lax.ppermute(lax.slice_in_dim(block, 0, width, axis=dim), axis, backward)]
    all_to_all x9 -> x0, local copies, waits for them, and re-layouts: 1.29 us -> none  [the longest x4 0.63 us: to_columns(): lax.all_to_all(grid_field, 'gx', split_axis=3, concat_axis=2, tiled=True)]
  transfers between devices with their start and end apart: 11 -> 0, of which waited for: 6 -> 0; matrix products, arithmetic and copies ran while one was open for 28% -> 0% of each run, Pallas kernels for 0% -> 0%
where the time goes in v1:
time: 17.2 us; the launch traced here: 16.9 us
  Pallas kernels  13.5 us (78%)
  local copies, waits for them, and re-layouts  2.77 us (16%)
  between operations  0.65 us (4%)
    pallas_call x1, Pallas kernels, on_device(): pl.pallas_call(functools.partial(kernel, groups, blocks), out_shape=[jax....  13.5 us
    unnamed x7, local copies, waits for them, and re-layouts  2.77 us

profile of v1, /device:TPU:0, one launch (start us, length us, event | category | flops | bytes accessed | tf_op | source)
XLA Modules:
  0.0 16.9 jit_solution(2900283896412668574)
XLA Ops:
  0.6 13.5 %step.1 = (f32[2,2,16,32]{3,2,1,0:T(8,128)}, f32[2,2,16,32]{3,2,1,0:T(8,128)}, f32[2,2,16,32]{3,2,1,0:T(8,128)}) custom-call(f32[2,2,16,32]{3,2,1,0:T(8,128)} %bitcast.11, f32[2,2,16,32]{3,2,1,0:T(8,128)} %bitcast.12, f32[8,128]{1,0:T(8,128)} %bitcast.16, f32[8,128]{1,0:T(8,128)} %bitcast.17, f32[8,128]{1,0:T(8,128)} %bitcast.18, s32[8,128]{1,0:T(8,128)} %bitcast.19, ...), custom_call_target="tpu_custom_call" | custom-call | tf_op jit(solution)/shard_map/step/pallas_call | solution.py:356
  14.1 0.0 copy-start.1
  14.2 1.4 %copy.14 = f32[2,32,2,16]{1,3,2,0:T(8,128)} copy(f32[2,32,2,16]{1,3,2,0:T(8,128)} %bitcast.15) | data formatting | bytes 16384
  15.5 0.0 copy-done.1
  15.5 0.0 copy-start
  15.5 0.6 %copy.15 = f32[2,32,2,16]{1,3,2,0:T(8,128)} copy(f32[2,32,2,16]{1,3,2,0:T(8,128)S(1)} %bitcast.14) | data formatting | bytes 16384
  16.2 0.2 copy-done
  16.3 0.6 %copy.16 = f32[2,32,2,16]{1,3,2,0:T(8,128)} copy(f32[2,32,2,16]{1,3,2,0:T(8,128)S(1)} %bitcast.13) | data formatting | bytes 16384
Async XLA Ops:
  14.1 1.4 %copy-start.1 = (f32[2,2,16,32]{3,2,1,0:T(8,128)S(1)}, f32[2,2,16,32]{3,2,1,0:T(8,128)}, u32[]{:S(2)}) copy-start(f32[2,2,16,32]{3,2,1,0:T(8,128)} %get-tuple-element.7) | copy-start | bytes 24580
  15.5 0.8 %copy-start = (f32[2,2,16,32]{3,2,1,0:T(8,128)S(1)}, f32[2,2,16,32]{3,2,1,0:T(8,128)}, u32[]{:S(2)}) copy-start(f32[2,2,16,32]{3,2,1,0:T(8,128)} %get-tuple-element.8) | copy-start | bytes 24580

commit v2 on v1

--- a/solution.py
+++ b/solution.py
@@ -341,6 +341,17 @@
         pl.loop(1, groups)(lambda d: pay_copy(d).wait_send())
 
 
+def write_out(next_v, vgrad_v, agrad_v, next_o, vgrad_o, agrad_o, sem):
+    copies = [
+        pltpu.make_async_copy(a, b, sem.at[i])
+        for i, (a, b) in enumerate(((next_v, next_o), (vgrad_v, vgrad_o), (agrad_v, agrad_o)))
+    ]
+    for copy in copies:
+        copy.start()
+    for copy in copies:
+        copy.wait()
+
+
 def on_device(groups, blocks, value, avoid, weight, offy, offs, xy, hs, count):
     slots = weight.shape[3]
     value = jnp.transpose(value, (0, 2, 3, 1))
@@ -355,8 +366,8 @@
     h_pair = pltpu.VMEM((2, cells, lines, speeds), f32)
     outs = pl.pallas_call(
         functools.partial(kernel, groups, blocks),
-        out_shape=[jax.ShapeDtypeStruct(value.shape, f32)] * 3,
-        in_specs=[pl.BlockSpec(memory_space=pl.ANY)] * 8,
+        out_shape=[pltpu.VMEM(value.shape, f32)] * 3,
+        in_specs=[pl.BlockSpec(memory_space=pltpu.HBM)] * 8,
         out_specs=[pl.BlockSpec(memory_space=pltpu.VMEM)] * 3,
         scratch_shapes=[
             field, field,
@@ -372,6 +383,15 @@
         compiler_params=pltpu.CompilerParams(collective_id=0, has_side_effects=True),
         name="step",
     )(value, avoid, weight, offy, offs, xy, hs, count)
+    outs = pl.pallas_call(
+        write_out,
+        out_shape=[jax.ShapeDtypeStruct(value.shape, f32)] * 3,
+        in_specs=[pl.BlockSpec(memory_space=pl.ANY)] * 3,
+        out_specs=[pl.BlockSpec(memory_space=pl.ANY)] * 3,
+        scratch_shapes=[dma((3,))],
+        compiler_params=pltpu.CompilerParams(vmem_limit_bytes=1 << 20),
+        name="write_out",
+    )(*outs)
     return tuple(jnp.transpose(o, (0, 3, 1, 2)) for o in outs)
 
 

time: 17.2 us -> 14.4 us (0.84)
  local copies, waits for them, and re-layouts: 2.77 us -> 0 us
    unnamed x7 -> x0, local copies, waits for them, and re-layouts: 2.77 us -> none
    pallas_call x1 -> x2, Pallas kernels: 13.5 us -> 13.5 us  [the longest x1 12.9 us: on_device(): pl.pallas_call(functools.partial(kernel, groups, blocks), out_shape=[pltp...]
where the time goes in v2:
time: 14.4 us; the launch traced here: 14.2 us
  Pallas kernels  13.5 us (94%)
  between operations  0.64 us (4%)
    pallas_call x1, Pallas kernels, on_device(): pl.pallas_call(functools.partial(kernel, groups, blocks), out_shape=[pltp...  12.9 us
    pallas_call x1, Pallas kernels, on_device(): pl.pallas_call(write_out, out_shape=[jax.ShapeDtypeStruct(value.shape, f3...  0.67 us

profile of v2, /device:TPU:0, one launch (start us, length us, event | category | flops | bytes accessed | tf_op | source)
XLA Modules:
  0.0 14.2 jit_solution(4992920561207016875)
XLA Ops:
  0.6 12.9 %step.1 = (f32[2,2,16,32]{3,2,1,0:T(8,128)S(1)}, f32[2,2,16,32]{3,2,1,0:T(8,128)S(1)}, f32[2,2,16,32]{3,2,1,0:T(8,128)S(1)}) custom-call(f32[2,2,16,32]{3,2,1,0:T(8,128)} %bitcast.11, f32[2,2,16,32]{3,2,1,0:T(8,128)} %bitcast.12, f32[8,128]{1,0:T(8,128)} %bitcast.13, f32[8,128]{1,0:T(8,128)} %bitcast.14, f32[8,128]{1,0:T(8,128)} %bitcast.15, ...), custom_call_target="tpu_custom_call" | custom-call | tf_op jit(solution)/shard_map/step/pallas_call | solution.py:367
  13.5 0.7 %write_out.1 = (f32[2,2,16,32]{3,2,1,0:T(8,128)}, f32[2,2,16,32]{3,2,1,0:T(8,128)}, f32[2,2,16,32]{3,2,1,0:T(8,128)}) custom-call(f32[2,2,16,32]{3,2,1,0:T(8,128)S(1)} %get-tuple-element.9.next_v, f32[2,2,16,32]{3,2,1,0:T(8,128)S(1)} %get-tuple-element.10.vgrad_v, f32[2,2,16,32]{3,2,1,0:T(8,128)S(1)} %get-tuple-element.11.agrad_v), custom_call_target="tpu_custom_call" | custom-call | tf_op jit(solution)/shard_map/write_out/pallas_call | solution.py:386

commit v3 on v2

--- a/solution.py
+++ b/solution.py
@@ -120,18 +120,19 @@
     pay[:, 6, :] = jnp.zeros((groups, slots), jnp.float32)
     pay[:, 7, :] = jnp.zeros((groups, slots), jnp.float32)
 
+    loads[6].wait()
     pl.semaphore_wait(barrier, groups - 1 + 2)
 
     def h_copy(side):
         return pltpu.make_async_remote_copy(
-            value_h.at[0 if side == 0 else heads - 1], hhalo.at[1 - side],
+            value.at[0 if side == 0 else heads - 1], hhalo.at[1 - side],
             h_send.at[side], h_recv.at[1 - side],
             device_id=(me, h_prev if side == 0 else h_next), device_id_type=MESH,
         )
 
     def x_copy(side):
         return pltpu.make_async_remote_copy(
-            value_h.at[:, 0 if side == 0 else cells - 1], xhalo.at[1 - side],
+            value.at[:, 0 if side == 0 else cells - 1], xhalo.at[1 - side],
             x_send.at[side], x_recv.at[1 - side],
             device_id=(me - 1 if side == 0 else me + 1, hb), device_id_type=MESH,
         )
@@ -157,7 +158,6 @@
         pl.loop(1, groups)(lambda d: pay_copy(d).start())
     mine = pltpu.make_async_copy(pay.at[me], got.at[0], self_sem)
     mine.start()
-    loads[6].wait()
     loads[7].wait()
 
     for side, has in ((0, has_prev), (1, has_next)):
@@ -200,7 +200,7 @@
         v[h, -1] = xhalo[0, h]
         v[h, cells] = xhalo[1, h]
 
-    share, h_slope = {}, {}
+    share, h_slope, above = {}, {}, {}
     for h, x in grid:
         here = v[h, x]
         up, down = v[h + 1, x], v[h - 1, x]
@@ -214,12 +214,8 @@
         floor = avoid[h, x]
         excess = SHARPNESS * (relaxed - floor)
         small = jnp.exp(-jnp.abs(excess))
-        next_o[h, x] = floor + (jnp.maximum(excess, 0.0) + jnp.log1p(small)) / SHARPNESS
-        inverse = 1.0 / (1.0 + small)
-        positive = excess >= 0.0
-        share[h, x] = (
-            jnp.where(positive, 1.0, small) * inverse, jnp.where(positive, small, 1.0) * inverse
-        )
+        share[h, x] = jnp.where(excess >= 0.0, 1.0, small) / (1.0 + small)
+        above[h, x] = (excess, small)
 
     rows = heads * cells * lines
     row_id = lax.broadcasted_iota(jnp.int32, (rows, slots), 0).astype(jnp.float32)
@@ -256,12 +252,12 @@
             jnp.zeros((rows, speeds), jnp.float32),
         )
 
-    c = {}
+    c, adj = {}, {}
     for n, (h, x) in enumerate(grid):
         adjoint = deposit[n * lines : (n + 1) * lines]
-        c[h, x] = adjoint * share[h, x][0]
+        c[h, x] = adjoint * share[h, x]
         carried[h, x] = c[h, x]
-        agrad_o[h, x] = adjoint * share[h, x][1]
+        adj[h, x] = adjoint
     ahead, back = {}, {}
     for h, x in grid:
         pull = (0.5 * TURN_RATE) * c[h, x] * h_slope[h, x]
@@ -298,6 +294,9 @@
 
     local = {}
     for h, x in grid:
+        excess, small = above[h, x]
+        next_o[h, x] = avoid[h, x] + (jnp.maximum(excess, 0.0) + jnp.log1p(small)) / SHARPNESS
+        agrad_o[h, x] = adj[h, x] * (jnp.where(excess >= 0.0, small, 1.0) / (1.0 + small))
         here = c[h, x]
         grad = spread((0.5 * cy[h] - 0.5) * here, (-0.5 * cy[h] - 0.5) * here, 0)
         pull = (0.5 * ACCELERATION) * here * s_slope[h, x]

time: 14.4 us -> 14.1 us (0.979)
  Pallas kernels: 13.5 us -> 13.3 us
    pallas_call x1, Pallas kernels: 12.9 us -> 12.6 us  [on_device(): pl.pallas_call(functools.partial(kernel, groups, blocks), out_shape=[pltp...]
where the time goes in v3:
time: 14.1 us; the launch traced here: 13.9 us
  Pallas kernels  13.3 us (94%)
  between operations  0.64 us (5%)
    pallas_call x1, Pallas kernels, on_device(): pl.pallas_call(functools.partial(kernel, groups, blocks), out_shape=[pltp...  12.6 us
    pallas_call x1, Pallas kernels, on_device(): pl.pallas_call(write_out, out_shape=[jax.ShapeDtypeStruct(value.shape, f3...  0.67 us

profile of v3, /device:TPU:0, one launch (start us, length us, event | category | flops | bytes accessed | tf_op | source)
XLA Modules:
  0.0 13.9 jit_solution(17100363370614329290)
XLA Ops:
  0.6 12.6 %step.1 = (f32[2,2,16,32]{3,2,1,0:T(8,128)S(1)}, f32[2,2,16,32]{3,2,1,0:T(8,128)S(1)}, f32[2,2,16,32]{3,2,1,0:T(8,128)S(1)}) custom-call(f32[2,2,16,32]{3,2,1,0:T(8,128)} %bitcast.11, f32[2,2,16,32]{3,2,1,0:T(8,128)} %bitcast.12, f32[8,128]{1,0:T(8,128)} %bitcast.13, f32[8,128]{1,0:T(8,128)} %bitcast.14, f32[8,128]{1,0:T(8,128)} %bitcast.15, ...), custom_call_target="tpu_custom_call" | custom-call | tf_op jit(solution)/shard_map/step/pallas_call | solution.py:366
  13.3 0.7 %write_out.1 = (f32[2,2,16,32]{3,2,1,0:T(8,128)}, f32[2,2,16,32]{3,2,1,0:T(8,128)}, f32[2,2,16,32]{3,2,1,0:T(8,128)}) custom-call(f32[2,2,16,32]{3,2,1,0:T(8,128)S(1)} %get-tuple-element.9.next_v, f32[2,2,16,32]{3,2,1,0:T(8,128)S(1)} %get-tuple-element.10.vgrad_v, f32[2,2,16,32]{3,2,1,0:T(8,128)S(1)} %get-tuple-element.11.agrad_v), custom_call_target="tpu_custom_call" | custom-call | tf_op jit(solution)/shard_map/write_out/pallas_call | solution.py:385

commit v4 on v3

--- a/solution.py
+++ b/solution.py
@@ -258,6 +258,21 @@
         c[h, x] = adjoint * share[h, x]
         carried[h, x] = c[h, x]
         adj[h, x] = adjoint
+    def cx_copy(side):
+        return pltpu.make_async_remote_copy(
+            carried.at[:, 0 if side == 0 else cells - 1], cxhalo.at[1 - side],
+            cx_send.at[side], cx_recv.at[1 - side],
+            device_id=(me - 1 if side == 0 else me + 1, hb), device_id_type=MESH,
+        )
+
+    for side, has in ((0, has_prev), (1, has_next)):
+        @pl.when(has)
+        def _():
+            cx_copy(side).start()
+
+        @pl.when(jnp.logical_not(has))
+        def _():
+            cxhalo[side] = jnp.zeros_like(cxhalo[side])
     ahead, back = {}, {}
     for h, x in grid:
         pull = (0.5 * TURN_RATE) * c[h, x] * h_slope[h, x]
@@ -274,21 +289,6 @@
             device_id=(me, h_prev if side == 0 else h_next), device_id_type=MESH,
         )
 
-    def cx_copy(side):
-        return pltpu.make_async_remote_copy(
-            carried.at[:, 0 if side == 0 else cells - 1], cxhalo.at[1 - side],
-            cx_send.at[side], cx_recv.at[1 - side],
-            device_id=(me - 1 if side == 0 else me + 1, hb), device_id_type=MESH,
-        )
-
-    for side, has in ((0, has_prev), (1, has_next)):
-        @pl.when(has)
-        def _():
-            cx_copy(side).start()
-
-        @pl.when(jnp.logical_not(has))
-        def _():
-            cxhalo[side] = jnp.zeros_like(cxhalo[side])
     for side in range(2):
         ch_copy(side).start()
 

time: 14.1 us -> 14.1 us (level)
  no operation moved by 1% of the time
where the time goes in v4:
time: 14.1 us; the launch traced here: 13.9 us
  Pallas kernels  13.3 us (94%)
  between operations  0.64 us (5%)
    pallas_call x1, Pallas kernels, on_device(): pl.pallas_call(functools.partial(kernel, groups, blocks), out_shape=[pltp...  12.6 us
    pallas_call x1, Pallas kernels, on_device(): pl.pallas_call(write_out, out_shape=[jax.ShapeDtypeStruct(value.shape, f3...  0.67 us

profile of v4, /device:TPU:0, one launch (start us, length us, event | category | flops | bytes accessed | tf_op | source)
XLA Modules:
  0.0 13.9 jit_solution(306861544614246351)
XLA Ops:
  0.6 12.6 %step.1 = (f32[2,2,16,32]{3,2,1,0:T(8,128)S(1)}, f32[2,2,16,32]{3,2,1,0:T(8,128)S(1)}, f32[2,2,16,32]{3,2,1,0:T(8,128)S(1)}) custom-call(f32[2,2,16,32]{3,2,1,0:T(8,128)} %bitcast.11, f32[2,2,16,32]{3,2,1,0:T(8,128)} %bitcast.12, f32[8,128]{1,0:T(8,128)} %bitcast.13, f32[8,128]{1,0:T(8,128)} %bitcast.14, f32[8,128]{1,0:T(8,128)} %bitcast.15, ...), custom_call_target="tpu_custom_call" | custom-call | tf_op jit(solution)/shard_map/step/pallas_call | solution.py:366
  13.3 0.7 %write_out.1 = (f32[2,2,16,32]{3,2,1,0:T(8,128)}, f32[2,2,16,32]{3,2,1,0:T(8,128)}, f32[2,2,16,32]{3,2,1,0:T(8,128)}) custom-call(f32[2,2,16,32]{3,2,1,0:T(8,128)S(1)} %get-tuple-element.9.next_v, f32[2,2,16,32]{3,2,1,0:T(8,128)S(1)} %get-tuple-element.10.vgrad_v, f32[2,2,16,32]{3,2,1,0:T(8,128)S(1)} %get-tuple-element.11.agrad_v), custom_call_target="tpu_custom_call" | custom-call | tf_op jit(solution)/shard_map/write_out/pallas_call | solution.py:385
